TPU v7x, 32 devices: a whole 2x2x4 slice. The times are simulated.
32 devices in a mesh: dp: 4 (over y, core), cells: 8 (over z, x).
Axes of the slice: x: 2, y: 2, z: 4, core: 2. Of those that a mesh axis runs over, the one named last changes fastest.
Arguments:
- sensitivity: float32 [8192, 12288], P('dp', 'cells'), may hold values from -0.0546875 to 0.0546875
- observed: float32 [8192, 256], P('dp'), may hold values from -6 to 6
- models: float32 [12288, 256], P('cells'), may hold values from -6 to 6
- neighbour_map: int32 [4, 768], replicated, may hold values from 0 to 767, as said below
- edge_mask: int32 [12288], P('cells'), may hold values 0 or 1
Outputs:
- updated: float32 [12288, 256], P('cells')
Inputs may be any that keep to these rules, and one draw needn't show every extreme that they name: `neighbour_map`: each row k maps every cell of a periodic 32 by 24 plane grid, numbered in a drawn order, to its neighbour in one of the four grid directions; every row is a permutation.
All inputs are finite; a program needn't handle non-finite values. No bound on the sum of `edge_mask` on one device may be relied on, other than what follows from the above.
Results may differ from a plain program's by a relative error of at most 0.0001.
Values sent between devices are 32-bit elements; how exact they have to be, the bound alone decides.
A program may use at most 128 MiB of HBM per device.

v0:
```python
import jax
import jax.numpy as jnp
from jax import lax
from jax.sharding import PartitionSpec as P

ITERS = 2


def with_halo(cells, sides, width):
    for axis, dim in sides:
        count = lax.axis_size(axis)
        ends = count - 1
        head = lax.slice_in_dim(cells, 0, width, axis=dim)
        tail = lax.slice_in_dim(cells, cells.shape[dim] - width, cells.shape[dim], axis=dim)
        cells = jnp.concatenate(
            [
                lax.ppermute(tail, axis, [(i, (i + 1) % count) for i in range(ends)]),
                cells,
                lax.ppermute(head, axis, [((i + 1) % count, i) for i in range(ends)]),
            ],
            axis=dim,
        )
    return cells


def reweight(misfit):
    return misfit / jnp.maximum(jnp.abs(misfit), 1.0)


def smooth_local(current, neighbour_map, edge_mask):
    plane_cells = neighbour_map.shape[1]
    count = current.shape[0] // plane_cells
    planes = current.reshape(count, plane_cells, current.shape[1])
    padded = with_halo(planes, (("cells", 0),), 1)
    total = jnp.zeros_like(planes)
    for other in (padded[:-2], padded[2:]):
        diff = other - planes
        total = total + diff / jnp.sqrt(1.0 + diff * diff)
    for k in range(4):
        other = jnp.take(planes, neighbour_map[k], axis=1)
        diff = other - planes
        total = total + diff / jnp.sqrt(1.0 + diff * diff)
    scale = 1.0 - 0.75 * edge_mask.astype(jnp.float32).reshape(count, plane_cells, 1)
    return (total * scale).reshape(current.shape)


def local(sensitivity, observed, models, neighbour_map, edge_mask):
    current = models
    for step in range(ITERS):
        predicted = lax.psum(
            jnp.dot(
                sensitivity,
                current,
                precision=lax.Precision.HIGHEST,
                preferred_element_type=jnp.float32,
            ),
            "cells",
        )
        weighted = reweight(predicted - observed)
        smooth = smooth_local(current, neighbour_map, edge_mask)
        partial_grad = lax.dot_general(
            sensitivity,
            weighted,
            (((0,), (0,)), ((), ())),
            precision=lax.Precision.HIGHEST,
            preferred_element_type=jnp.float32,
        )
        gradient = lax.psum(partial_grad, "dp")
        current = current - 1.0 * gradient + 0.05 * smooth
    return current


def solution(mesh):
    return jax.shard_map(
        local,
        mesh=mesh,
        in_specs=(P("dp", "cells"), P("dp", None), P("cells", None), P(), P("cells")),
        out_specs=P("cells", None),
        check_vma=False,
    )
```

profile of v0, /device:TPU:0, one launch (start us, length us, event | category | flops | bytes accessed | tf_op | source)
XLA Modules:
  0.0 418.7 jit_solution(4675436302633939359)
XLA Ops:
  6.5 13.9 %fusion.16 = f32[2048,256]{1,0:T(8,128)} fusion(f32[2048,1536]{1,0:T(8,128)} %param.7, f32[1536,256]{1,0:T(8,128)} %param.9), kind=kOutput, calls=%fused_computation.72 | convolution fusion | flops 9663676416 | bytes 16252928 | tf_op jit(solution)/shard_map/dot_general | solution.py:51
  20.6 1.3 copy-done
  21.9 1.3 slice_bitcast_fusion.3
  23.1 5.7 %collective-permute-start = (f32[1,768,256]{2,1,0:T(8,128)}, f32[1,768,256]{2,1,0:T(8,128)}, u32[]{:S(2)}, u32[]{:S(2)}) collective-permute-start(f32[1,768,256]{2,1,0:T(8,128)} %get-tuple-element.12), channel_id=1, source_target_pairs={{0,1},{1,2},{2,3},{3,4},{4,5},{5,6},{6,7},{8,9},{9,10},{10,11},{11... | collective-permute-start | bytes 2359304 | tf_op jit(solution)/shard_map/ppermute | solution.py:17
  28.9 1.3 collective-permute-start.1
  30.2 1.2 copy.73
  31.5 4.0 gather_fusion.3
  35.5 4.0 gather_fusion.2
  39.6 4.0 gather_fusion.1
  43.6 4.1 gather_fusion
  47.7 96.1 %all-reduce.5.cloned.1.call-done = f32[2048,256]{1,0:T(8,128)} async-done(((f32[2048,256]{1,0:T(8,128)}), f32[2048,256]{1,0:T(8,128)}) %all-reduce.5.cloned.1.call-update) | async-done | bytes 2097168 | tf_op jit(solution)/shard_map/psum | solution.py:50
  143.8 25.0 %convolution_bitcast_fusion.2 = f32[1536,256]{1,0:T(8,128)} fusion(f32[2048,1536]{1,0:T(8,128)} %param.7, f32[2048,256]{1,0:T(8,128)} %all-reduce.5.cloned.1.call-done, f32[2048,256]{1,0:T(8,128)} %param.8), kind=kOutput, calls=%fused_computation.10 | convolution fusion | flops 9665773568 | bytes 18350080 | tf_op jit(solution)/shard_map/dot_general | solution.py:61
  168.8 0.0 all-reduce.9.cloned.1.call-start
  168.9 1.3 copy-done.1
  170.2 6.2 %multiply_multiply_fusion.1 = f32[2,768,256]{2,1,0:T(8,128)} fusion(f32[2,768,256]{2,1,0:T(8,128)S(1)} %bitcast.61, f32[768,2,256]{2,1,0:T(2,128)S(1)} %copy-done.1, f32[768,2,256]{2,1,0:T(2,128)} %gather_fusion.2, f32[768,2,256]{2,1,0:T(2,128)} %gather_fusion.1, f32[768,2,256]{2,1,0:T(2,128)} %gather_fusion, f32[1,768,256]{2,1,0:T(8,128)} %collective-permute-done.1, ...), kind=kLoop, calls=%fused_computation.46 | loop fusion | flops 14548992 | bytes 11019264 | tf_op jit(solution)/shard_map/mul | solution.py:69
  176.4 34.7 %all-reduce.7.cloned.1.call-done = f32[1536,256]{1,0:T(8,128)} async-done(((f32[1536,256]{1,0:T(8,128)}), f32[1536,256]{1,0:T(8,128)}) %all-reduce.7.cloned.1.call-update) | async-done | bytes 1572880 | tf_op jit(solution)/shard_map/psum | solution.py:68
  211.1 2.2 bitcast_add_fusion.1
  213.3 13.5 %convolution_bitcast_fusion.1 = f32[2048,256]{1,0:T(8,128)} fusion(f32[1536,256]{1,0:T(8,128)S(1)} %bitcast_add_fusion.1, f32[2048,1536]{1,0:T(8,128)} %param.7), kind=kOutput, calls=%fused_computation.9 | convolution fusion | flops 9663676416 | bytes 16252928 | tf_op jit(solution)/shard_map/dot_general | solution.py:51
  226.9 1.2 copy.83
  228.1 4.0 gather_fusion.7
  232.1 4.0 gather_fusion.6
  236.1 4.0 gather_fusion.5
  240.2 4.1 gather_fusion.4
  244.2 1.3 slice_bitcast_fusion.1
  245.5 4.2 %collective-permute-start.2 = (f32[1,768,256]{2,1,0:T(8,128)}, f32[1,768,256]{2,1,0:T(8,128)}, u32[]{:S(2)}, u32[]{:S(2)}) collective-permute-start(f32[1,768,256]{2,1,0:T(8,128)} %get-tuple-element.10), channel_id=1, source_target_pairs={{0,1},{1,2},{2,3},{3,4},{4,5},{5,6},{6,7},{8,9},{9,10},{10,11},{11... | collective-permute-start | bytes 2359304 | tf_op jit(solution)/shard_map/ppermute | solution.py:17
  249.7 1.3 collective-permute-start.3
  251.0 90.5 %all-reduce.9.cloned.1.call-done = f32[2048,256]{1,0:T(8,128)} async-done(((f32[2048,256]{1,0:T(8,128)}), f32[2048,256]{1,0:T(8,128)}) %all-reduce.9.cloned.1.call-update) | async-done | bytes 2097168 | tf_op jit(solution)/shard_map/psum | solution.py:50
  341.5 24.8 %convolution_bitcast_fusion = f32[1536,256]{1,0:T(8,128)} fusion(f32[2048,1536]{1,0:T(8,128)} %param.7, f32[2048,256]{1,0:T(8,128)} %all-reduce.9.cloned.1.call-done, f32[2048,256]{1,0:T(8,128)} %param.8), kind=kOutput, calls=%fused_computation.8 | convolution fusion | flops 9665773568 | bytes 18350080 | tf_op jit(solution)/shard_map/dot_general | solution.py:61
  366.3 1.4 copy-done.2
  367.7 6.1 %multiply_multiply_fusion = f32[2,768,256]{2,1,0:T(8,128)} fusion(f32[2,768,256]{2,1,0:T(8,128)S(1)} %bitcast.59, f32[768,2,256]{2,1,0:T(2,128)S(1)} %copy-done.2, f32[768,2,256]{2,1,0:T(2,128)} %gather_fusion.6, f32[768,2,256]{2,1,0:T(2,128)} %gather_fusion.5, f32[768,2,256]{2,1,0:T(2,128)} %gather_fusion.4, f32[1,768,256]{2,1,0:T(8,128)} %collective-permute-done.3, ...), kind=kLoop, calls=%fused_computation.45 | loop fusion | flops 14548992 | bytes 11019264 | tf_op jit(solution)/shard_map/mul | solution.py:69
  373.8 34.8 %all-reduce.11.cloned.1.call-done = f32[1536,256]{1,0:T(8,128)} async-done(((f32[1536,256]{1,0:T(8,128)}), f32[1536,256]{1,0:T(8,128)}) %all-reduce.11.cloned.1.call-update) | async-done | bytes 1572880 | tf_op jit(solution)/shard_map/psum | solution.py:68
  408.6 3.3 bitcast_add_fusion
  (29 shorter events, 0.3 us)
Async XLA Ops:
  6.5 137.2 %all-reduce.5.cloned.1.call-start = ((), (), s32[]{:S(2)}) async-start(), calls=%async_computation | async-start | bytes 4194304 | tf_op jit(solution)/shard_map/psum | solution.py:50
  20.5 1.4 copy-start
  20.5 9.7 %copy-start.4 = (s32[1536]{0:T(1024)S(1)}, s32[1536]{0:T(1024)}, u32[]{:S(2)}) copy-start(s32[1536]{0:T(1024)} %param.11) | copy-start | bytes 18436
  20.5 190.6 %all-reduce.7.cloned.1.call-start = ((), (), s32[]{:S(2)}) async-start(), calls=%async_computation.1 | async-start | bytes 3145728 | tf_op jit(solution)/shard_map/psum | solution.py:68
  23.1 145.7 %collective-permute-start = (f32[1,768,256]{2,1,0:T(8,128)}, f32[1,768,256]{2,1,0:T(8,128)}, u32[]{:S(2)}, u32[]{:S(2)}) collective-permute-start(f32[1,768,256]{2,1,0:T(8,128)} %get-tuple-element.12), channel_id=1, source_target_pairs={{0,1},{1,2},{2,3},{3,4},{4,5},{5,6},{6,7},{8,9},{9,10},{10,11},{11... | collective-permute-start | bytes 2359304 | tf_op jit(solution)/shard_map/ppermute | solution.py:17
  28.9 140.0 %collective-permute-start.1 = (f32[1,768,256]{2,1,0:T(8,128)}, f32[1,768,256]{2,1,0:T(8,128)}, u32[]{:S(2)}, u32[]{:S(2)}) collective-permute-start(f32[1,768,256]{2,1,0:T(8,128)} %get-tuple-element.13), channel_id=1, source_target_pairs={{1,0},{2,1},{3,2},{4,3},{5,4},{6,5},{7,6},{9,8},{10,9},{11,10},{12... | collective-permute-start | bytes 2359304 | tf_op jit(solution)/shard_map/ppermute | solution.py:19
  30.2 1.2 copy-start.3
  168.8 1.4 copy-start.1
  168.8 172.7 %all-reduce.9.cloned.1.call-start = ((), (), s32[]{:S(2)}) async-start(), calls=%async_computation.2 | async-start | bytes 4194304 | tf_op jit(solution)/shard_map/psum | solution.py:50
  226.8 181.8 %all-reduce.11.cloned.1.call-start = ((), (), s32[]{:S(2)}) async-start(), calls=%async_computation.3 | async-start | bytes 3145728 | tf_op jit(solution)/shard_map/psum | solution.py:68
  245.5 120.8 %collective-permute-start.2 = (f32[1,768,256]{2,1,0:T(8,128)}, f32[1,768,256]{2,1,0:T(8,128)}, u32[]{:S(2)}, u32[]{:S(2)}) collective-permute-start(f32[1,768,256]{2,1,0:T(8,128)} %get-tuple-element.10), channel_id=1, source_target_pairs={{0,1},{1,2},{2,3},{3,4},{4,5},{5,6},{6,7},{8,9},{9,10},{10,11},{11... | collective-permute-start | bytes 2359304 | tf_op jit(solution)/shard_map/ppermute | solution.py:17
  249.7 116.6 %collective-permute-start.3 = (f32[1,768,256]{2,1,0:T(8,128)}, f32[1,768,256]{2,1,0:T(8,128)}, u32[]{:S(2)}, u32[]{:S(2)}) collective-permute-start(f32[1,768,256]{2,1,0:T(8,128)} %get-tuple-element.11), channel_id=1, source_target_pairs={{1,0},{2,1},{3,2},{4,3},{5,4},{6,5},{7,6},{9,8},{10,9},{11,10},{12... | collective-permute-start | bytes 2359304 | tf_op jit(solution)/shard_map/ppermute | solution.py:19
  366.3 1.4 copy-start.2
Sparse Core Ops, SparseCore 0:
  20.6 123.1 all-reduce.4
  168.9 42.1 all-reduce.6
  227.0 114.5 all-reduce.8
  366.4 42.1 all-reduce.10
where the time goes:
time: 426 us; the launch traced here: 419 us
  waiting for transfers between devices  256 us (60%)
  matrix products  77.2 us (18%)
  local copies, waits for them, and re-layouts  41.2 us (10%)
  other arithmetic  17.9 us (4%)
  between operations  13.5 us (3%)
  starting transfers between devices  12.7 us (3%)
    psum x2, waiting for transfers between devices, local(): lax.psum(jnp.dot(sensitivity, current, precision=lax.Precision.HIGHEST, p...  187 us
    psum x2, waiting for transfers between devices, local(): gradient = lax.psum(partial_grad, 'dp')  69.5 us
    dot_general x2, matrix products, local(): lax.dot_general(sensitivity, weighted, (((0,), (0,)), ((), ())), precisio...  49.8 us
    gather x8, local copies, waits for them, and re-layouts, smooth_local(): other = jnp.take(planes, neighbour_map[k], axis=1)  32.2 us
    dot_general x2, matrix products, local(): jnp.dot(sensitivity, current, precision=lax.Precision.HIGHEST, preferred_...  27.5 us
    mul x2, other arithmetic, local(): current = current - 1.0 * gradient + 0.05 * smooth  12.3 us
    ppermute x2, starting transfers between devices, with_halo(): lax.ppermute(tail, axis, [(i, (i + 1) % count) for i in range(ends)])  9.98 us
  transfers between devices with their start and end apart: 8, of which 4 were waited for; matrix products, arithmetic and copies ran while one was open for 24% of the time, Pallas kernels for 0%

commit v1 on v0

--- a/solution.py
+++ b/solution.py
@@ -65,7 +65,10 @@
             precision=lax.Precision.HIGHEST,
             preferred_element_type=jnp.float32,
         )
-        gradient = lax.psum(partial_grad, "dp")
+        size, gradient = (lax.axis_size("dp"), partial_grad)
+        for stride in [1 << k_2 for k_2 in range(size.bit_length() - 1)]:
+            swap = [(i_2, i_2 ^ stride) for i_2 in range(size)]
+            gradient = gradient + lax.ppermute(gradient, "dp", swap)
         current = current - 1.0 * gradient + 0.05 * smooth
     return current
 

time: 426 us -> 405 us (0.951)
  waiting for transfers between devices: 256 us -> 238 us
    psum x2 -> x0, waiting for transfers between devices: 69.5 us -> none  [local(): gradient = lax.psum(partial_grad, 'dp')]
    ppermute x2, waiting for transfers between devices: 0.01 us -> 21.9 us  [with_halo(): lax.ppermute(tail, axis, [(i, (i + 1) % count) for i in range(ends)])]
    psum x2, waiting for transfers between devices: 187 us -> 207 us  [local(): lax.psum(jnp.dot(sensitivity, current, precision=lax.Precision.HIGHEST, p...]
    ppermute x0 -> x4, waiting for transfers between devices: none -> 8.9 us  [local(): gradient = gradient + lax.ppermute(gradient, 'dp', swap)]
    add x0 -> x2, other arithmetic: none -> 4.59 us  [local(): gradient = gradient + lax.ppermute(gradient, 'dp', swap)]
  transfers between devices with their start and end apart: 8 -> 10, of which waited for: 4 -> 6; matrix products, arithmetic and copies ran while one was open for 24% -> 13% of each run, Pallas kernels for 0% -> 0%
where the time goes in v1:
time: 405 us; the launch traced here: 402 us
  waiting for transfers between devices  238 us (59%)
  matrix products  76.4 us (19%)
  local copies, waits for them, and re-layouts  37.2 us (9%)
  other arithmetic  21.1 us (5%)
  starting transfers between devices  15.2 us (4%)
  between operations  13.8 us (3%)
    psum x2, waiting for transfers between devices, local(): lax.psum(jnp.dot(sensitivity, current, precision=lax.Precision.HIGHEST, p...  207 us
    dot_general x2, matrix products, local(): lax.dot_general(sensitivity, weighted, (((0,), (0,)), ((), ())), precisio...  48.9 us
    gather x8, local copies, waits for them, and re-layouts, smooth_local(): other = jnp.take(planes, neighbour_map[k], axis=1)  32 us
    dot_general x2, matrix products, local(): jnp.dot(sensitivity, current, precision=lax.Precision.HIGHEST, preferred_...  27.5 us
    ppermute x2, waiting for transfers between devices, with_halo(): lax.ppermute(tail, axis, [(i, (i + 1) % count) for i in range(ends)])  21.9 us
    mul x2, other arithmetic, local(): current = current - 1.0 * gradient + 0.05 * smooth  10.6 us
    ppermute x4, waiting for transfers between devices, local(): gradient = gradient + lax.ppermute(gradient, 'dp', swap)  8.9 us
    ppermute x2, starting transfers between devices, with_halo(): lax.ppermute(tail, axis, [(i, (i + 1) % count) for i in range(ends)])  8.56 us
  transfers between devices with their start and end apart: 10, of which 6 were waited for; matrix products, arithmetic and copies ran while one was open for 13% of the time, Pallas kernels for 0%

profile of v1, /device:TPU:0, one launch (start us, length us, event | category | flops | bytes accessed | tf_op | source)
XLA Modules:
  0.0 401.8 jit_solution(3334599808174801294)
XLA Ops:
  6.5 13.9 %fusion.16 = f32[2048,256]{1,0:T(8,128)} fusion(f32[2048,1536]{1,0:T(8,128)} %param.7, f32[1536,256]{1,0:T(8,128)} %param.9), kind=kOutput, calls=%fused_computation.72 | convolution fusion | flops 9663676416 | bytes 16252928 | tf_op jit(solution)/shard_map/dot_general | solution.py:51
  20.8 104.8 %all-reduce.3.cloned.1.call-done = f32[2048,256]{1,0:T(8,128)} async-done(((f32[2048,256]{1,0:T(8,128)}), f32[2048,256]{1,0:T(8,128)}) %all-reduce.3.cloned.1.call-update) | async-done | bytes 2097168 | tf_op jit(solution)/shard_map/psum | solution.py:50
  125.7 24.6 %convolution_bitcast_fusion.2 = f32[1536,256]{1,0:T(8,128)} fusion(f32[2048,1536]{1,0:T(8,128)} %param.7, f32[2048,256]{1,0:T(8,128)} %all-reduce.3.cloned.1.call-done, f32[2048,256]{1,0:T(8,128)} %param.8), kind=kOutput, calls=%fused_computation.10 | convolution fusion | flops 9665773568 | bytes 18350080 | tf_op jit(solution)/shard_map/dot_general | solution.py:61
  150.3 1.3 slice_bitcast_fusion.3
  151.6 4.3 %collective-permute-start.2 = (f32[1,768,256]{2,1,0:T(8,128)}, f32[1,768,256]{2,1,0:T(8,128)}, u32[]{:S(2)}, u32[]{:S(2)}) collective-permute-start(f32[1,768,256]{2,1,0:T(8,128)} %get-tuple-element.12), channel_id=1, source_target_pairs={{0,1},{1,2},{2,3},{3,4},{4,5},{5,6},{6,7},{8,9},{9,10},{10,11},{11... | collective-permute-start | bytes 2359304 | tf_op jit(solution)/shard_map/ppermute | solution.py:17
  155.9 1.8 collective-permute-start.3
  157.8 1.2 copy.73
  159.1 4.0 gather_fusion.3
  163.1 3.2 add.94
  166.3 1.5 collective-permute-start.1
  167.8 4.0 %gather_fusion.2 = f32[768,2,256]{2,1,0:T(2,128)} fusion(f32[2,768,256]{2,0,1:T(2,128)S(1)} %copy.73, s32[1024]{0:T(1024)S(1)} %pad_clamp_fusion.1), kind=kCustom, calls=%fused_computation.2.clone | custom fusion | bytes 3148800 | tf_op jit(solution)/shard_map/jit(_take)/gather | solution.py:40
  171.8 4.0 gather_fusion.1
  175.8 4.0 gather_fusion
  179.9 9.7 %collective-permute-done.2 = f32[1,768,256]{2,1,0:T(8,128)} collective-permute-done((f32[1,768,256]{2,1,0:T(8,128)}, f32[1,768,256]{2,1,0:T(8,128)}, u32[]{:S(2)}, u32[]{:S(2)}) %collective-permute-start.2) | collective-permute-done | bytes 786464 | tf_op jit(solution)/shard_map/ppermute | solution.py:17
  189.6 5.3 %multiply_multiply_fusion.1 = f32[2,768,256]{2,1,0:T(8,128)S(1)} fusion(f32[2,768,256]{2,1,0:T(8,128)S(1)} %bitcast.61, f32[768,2,256]{2,1,0:T(2,128)} %gather_fusion.3, f32[768,2,256]{2,1,0:T(2,128)} %gather_fusion.2, f32[768,2,256]{2,1,0:T(2,128)} %gather_fusion.1, f32[768,2,256]{2,1,0:T(2,128)} %gather_fusion, f32[1,768,256]{2,1,0:T(8,128)} %collective-permute-done.3, ...), kind=kLoop, calls=%fused_computation.46 | loop fusion | flops 14548992 | bytes 11019264 | tf_op jit(solution)/shard_map/mul | solution.py:72
  194.9 8.2 %collective-permute-done.1 = f32[1536,256]{1,0:T(8,128)} collective-permute-done((f32[1536,256]{1,0:T(8,128)}, f32[1536,256]{1,0:T(8,128)}, u32[]{:S(2)}, u32[]{:S(2)}) %collective-permute-start.1) | collective-permute-done | bytes 1572896 | tf_op jit(solution)/shard_map/ppermute | solution.py:71
  203.1 2.4 bitcast_add_fusion.1
  205.5 13.5 %convolution_bitcast_fusion.1 = f32[2048,256]{1,0:T(8,128)} fusion(f32[1536,256]{1,0:T(8,128)S(1)} %bitcast_add_fusion.1, f32[2048,1536]{1,0:T(8,128)} %param.7), kind=kOutput, calls=%fused_computation.9 | convolution fusion | flops 9663676416 | bytes 16252928 | tf_op jit(solution)/shard_map/dot_general | solution.py:51
  219.1 102.5 %all-reduce.5.cloned.1.call-done = f32[2048,256]{1,0:T(8,128)} async-done(((f32[2048,256]{1,0:T(8,128)}), f32[2048,256]{1,0:T(8,128)}) %all-reduce.5.cloned.1.call-update) | async-done | bytes 2097168 | tf_op jit(solution)/shard_map/psum | solution.py:50
  321.5 24.3 %convolution_bitcast_fusion = f32[1536,256]{1,0:T(8,128)S(1)} fusion(f32[2048,1536]{1,0:T(8,128)} %param.7, f32[2048,256]{1,0:T(8,128)} %all-reduce.5.cloned.1.call-done, f32[2048,256]{1,0:T(8,128)} %param.8), kind=kOutput, calls=%fused_computation.8 | convolution fusion | flops 9665773568 | bytes 18350080 | tf_op jit(solution)/shard_map/dot_general | solution.py:61
  346.0 1.3 slice_bitcast_fusion.1
  347.3 4.3 %collective-permute-start.6 = (f32[1,768,256]{2,1,0:T(8,128)}, f32[1,768,256]{2,1,0:T(8,128)}, u32[]{:S(2)}, u32[]{:S(2)}) collective-permute-start(f32[1,768,256]{2,1,0:T(8,128)} %get-tuple-element.10), channel_id=1, source_target_pairs={{0,1},{1,2},{2,3},{3,4},{4,5},{5,6},{6,7},{8,9},{9,10},{10,11},{11... | collective-permute-start | bytes 2359304 | tf_op jit(solution)/shard_map/ppermute | solution.py:17
  351.6 1.5 collective-permute-start.7
  353.1 1.4 add.108
  354.4 1.5 collective-permute-start.5
  357.1 4.0 gather_fusion.7
  361.1 4.0 gather_fusion.6
  365.1 4.0 gather_fusion.5
  369.2 4.0 gather_fusion.4
  373.1 12.1 %collective-permute-done.6 = f32[1,768,256]{2,1,0:T(8,128)} collective-permute-done((f32[1,768,256]{2,1,0:T(8,128)}, f32[1,768,256]{2,1,0:T(8,128)}, u32[]{:S(2)}, u32[]{:S(2)}) %collective-permute-start.6) | collective-permute-done | bytes 786464 | tf_op jit(solution)/shard_map/ppermute | solution.py:17
  385.3 5.3 %multiply_multiply_fusion = f32[2,768,256]{2,1,0:T(8,128)S(1)} fusion(f32[2,768,256]{2,1,0:T(8,128)S(1)} %bitcast.59, f32[768,2,256]{2,1,0:T(2,128)} %gather_fusion.7, f32[768,2,256]{2,1,0:T(2,128)} %gather_fusion.6, f32[768,2,256]{2,1,0:T(2,128)} %gather_fusion.5, f32[768,2,256]{2,1,0:T(2,128)} %gather_fusion.4, f32[1,768,256]{2,1,0:T(8,128)} %collective-permute-done.7, ...), kind=kLoop, calls=%fused_computation.45 | loop fusion | flops 14548992 | bytes 11019264 | tf_op jit(solution)/shard_map/mul | solution.py:72
  391.3 3.5 bitcast_add_fusion
  (29 shorter events, 2.5 us)
Async XLA Ops:
  6.5 119.1 %all-reduce.3.cloned.1.call-start = ((), (), s32[]{:S(2)}) async-start(), calls=%async_computation | async-start | bytes 4194304 | tf_op jit(solution)/shard_map/psum | solution.py:50
  20.5 129.8 %copy-start = (f32[1536,256]{1,0:T(8,128)S(1)}, f32[1536,256]{1,0:T(8,128)}, u32[]{:S(2)}) copy-start(f32[1536,256]{1,0:T(8,128)} %param.9) | copy-start | bytes 4718596
  20.5 301.0 %all-reduce.5.cloned.1.call-start = ((), (), s32[]{:S(2)}) async-start(), calls=%async_computation.1 | async-start | bytes 4194304 | tf_op jit(solution)/shard_map/psum | solution.py:50
  150.3 7.5 %copy-start.1 = (s32[4,768]{1,0:T(4,128)S(1)}, s32[4,768]{1,0:T(4,128)}, u32[]{:S(2)}) copy-start(s32[4,768]{1,0:T(4,128)} %param.10) | copy-start | bytes 36868
  150.3 7.5 %copy-start.2 = (s32[1536]{0:T(1024)S(1)}, s32[1536]{0:T(1024)}, u32[]{:S(2)}) copy-start(s32[1536]{0:T(1024)} %param.11) | copy-start | bytes 18436
  150.3 12.8 %collective-permute-start = (f32[1536,256]{1,0:T(8,128)}, f32[1536,256]{1,0:T(8,128)}, u32[]{:S(2)}, u32[]{:S(2)}) collective-permute-start(f32[1536,256]{1,0:T(8,128)} %convolution_bitcast_fusion.2), channel_id=1, source_target_pairs={{0,8},{8,0},{16,24},{24,16},{1,9},{9,1},{17,25},{25,17},{2,10},{10... | collective-permute-start | bytes 4718600 | tf_op jit(solution)/shard_map/ppermute | solution.py:71
  151.6 38.0 %collective-permute-start.2 = (f32[1,768,256]{2,1,0:T(8,128)}, f32[1,768,256]{2,1,0:T(8,128)}, u32[]{:S(2)}, u32[]{:S(2)}) collective-permute-start(f32[1,768,256]{2,1,0:T(8,128)} %get-tuple-element.12), channel_id=1, source_target_pairs={{0,1},{1,2},{2,3},{3,4},{4,5},{5,6},{6,7},{8,9},{9,10},{10,11},{11... | collective-permute-start | bytes 2359304 | tf_op jit(solution)/shard_map/ppermute | solution.py:17
  155.9 33.7 %collective-permute-start.3 = (f32[1,768,256]{2,1,0:T(8,128)}, f32[1,768,256]{2,1,0:T(8,128)}, u32[]{:S(2)}, u32[]{:S(2)}) collective-permute-start(f32[1,768,256]{2,1,0:T(8,128)} %get-tuple-element.13), channel_id=1, source_target_pairs={{1,0},{2,1},{3,2},{4,3},{5,4},{6,5},{7,6},{9,8},{10,9},{11,10},{12... | collective-permute-start | bytes 2359304 | tf_op jit(solution)/shard_map/ppermute | solution.py:19
  166.3 36.8 %collective-permute-start.1 = (f32[1536,256]{1,0:T(8,128)}, f32[1536,256]{1,0:T(8,128)}, u32[]{:S(2)}, u32[]{:S(2)}) collective-permute-start(f32[1536,256]{1,0:T(8,128)} %add.94), channel_id=1, source_target_pairs={{0,16},{8,24},{16,0},{24,8},{1,17},{9,25},{17,1},{25,9},{2,18},{10... | collective-permute-start | bytes 4718600 | tf_op jit(solution)/shard_map/ppermute | solution.py:71
  345.9 7.2 %collective-permute-start.4 = (f32[1536,256]{1,0:T(8,128)S(1)}, f32[1536,256]{1,0:T(8,128)S(1)}, u32[]{:S(2)}, u32[]{:S(2)}) collective-permute-start(f32[1536,256]{1,0:T(8,128)S(1)} %convolution_bitcast_fusion), channel_id=1, source_target_pairs={{0,8},{8,0},{16,24},{24,16},{1,9},{9,1},{17,25},{25,17},{2,10},{10... | collective-permute-start | bytes 4718600 | tf_op jit(solution)/shard_map/ppermute | solution.py:71
  347.3 38.0 %collective-permute-start.6 = (f32[1,768,256]{2,1,0:T(8,128)}, f32[1,768,256]{2,1,0:T(8,128)}, u32[]{:S(2)}, u32[]{:S(2)}) collective-permute-start(f32[1,768,256]{2,1,0:T(8,128)} %get-tuple-element.10), channel_id=1, source_target_pairs={{0,1},{1,2},{2,3},{3,4},{4,5},{5,6},{6,7},{8,9},{9,10},{10,11},{11... | collective-permute-start | bytes 2359304 | tf_op jit(solution)/shard_map/ppermute | solution.py:17
  351.6 33.7 %collective-permute-start.7 = (f32[1,768,256]{2,1,0:T(8,128)}, f32[1,768,256]{2,1,0:T(8,128)}, u32[]{:S(2)}, u32[]{:S(2)}) collective-permute-start(f32[1,768,256]{2,1,0:T(8,128)} %get-tuple-element.11), channel_id=1, source_target_pairs={{1,0},{2,1},{3,2},{4,3},{5,4},{6,5},{7,6},{9,8},{10,9},{11,10},{12... | collective-permute-start | bytes 2359304 | tf_op jit(solution)/shard_map/ppermute | solution.py:19
  354.4 36.8 %collective-permute-start.5 = (f32[1536,256]{1,0:T(8,128)}, f32[1536,256]{1,0:T(8,128)}, u32[]{:S(2)}, u32[]{:S(2)}) collective-permute-start(f32[1536,256]{1,0:T(8,128)} %add.108), channel_id=1, source_target_pairs={{0,16},{8,24},{16,0},{24,8},{1,17},{9,25},{17,1},{25,9},{2,18},{10... | collective-permute-start | bytes 4718600 | tf_op jit(solution)/shard_map/ppermute | solution.py:71
Sparse Core Ops, SparseCore 0:
  20.6 105.0 all-reduce.2
  219.2 102.3 all-reduce.4
